TPU v7x, 128 devices: a whole 4x4x4 slice. The times are simulated.
128 devices in a mesh: slab: 32 (over y, z, core), col: 4 (over x).
Axes of the slice: x: 4, y: 4, z: 4, core: 2. Of those that a mesh axis runs over, the one named last changes fastest.
Arguments:
- input_map: float32 [64, 64, 192, 128], P('col', 'slab'), may hold values from -24 to 24
- output_map: float32 [64, 64, 192, 128], P('col', 'slab'), may hold values from -24 to 24
- region_ids: int32 [64, 192, 128], P('slab'), may hold values from 0 to 7
- region_cond: float32 [8], replicated, may hold values from 0.3 to 3
- shift_ids: int32 [2], replicated, may hold values from 0 to 7
Outputs:
- ctrl_factor: float32 [2, 64, 64, 192, 128], P(None, None, 'slab', 'col')
- obsv_factor: float32 [2, 64, 64, 192, 128], P(None, None, 'slab', 'col')
- cross_gram: float32 [128, 128], P('slab', 'col')
All inputs are finite; a program needn't handle non-finite values.
Results may differ from a plain program's by a relative error of at most 0.000098.
Values sent between devices are 32-bit elements; how exact they have to be, the bound alone decides.
A program may use at most 192 MiB of HBM per device.

v0:
```python
import math
import jax
import jax.numpy as jnp
from jax import lax
from jax.sharding import PartitionSpec as P

ADI = 2
STEPS = 3


def extended(block, sides, width):
    for axis, dim in sides:
        count = lax.axis_size(axis)
        forward = [(i, i + 1) for i in range(count - 1)]
        backward = [(target, source) for source, target in forward]
        low = lax.ppermute(
            lax.slice_in_dim(block, block.shape[dim] - width, None, axis=dim), axis, forward
        )
        high = lax.ppermute(lax.slice_in_dim(block, 0, width, axis=dim), axis, backward)
        block = jnp.concatenate([low, block, high], axis=dim)
    return block


def lookup(region_ids, region_cond):
    summed = jnp.zeros(region_ids.shape, jnp.float32)
    for region in range(region_cond.shape[0]):
        summed = summed + jnp.where(region_ids == region, region_cond[region], jnp.float32(0.0))
    return summed


def conduction(field_in, cond_ext):
    centre = field_in[:, 1:-1]
    cond_mid = cond_ext[1:-1]
    summed = 0.5 * (cond_mid + cond_ext[2:]) * (centre - field_in[:, 2:])
    summed = summed + 0.5 * (cond_mid + cond_ext[:-2]) * (centre - field_in[:, :-2])
    cond_y = jnp.pad(cond_mid, ((0, 0), (1, 1), (0, 0)))
    field_y = jnp.pad(centre, ((0, 0), (0, 0), (1, 1), (0, 0)))
    summed = summed + 0.5 * (cond_mid + cond_y[:, 2:]) * (centre - field_y[:, :, 2:])
    summed = summed + 0.5 * (cond_mid + cond_y[:, :-2]) * (centre - field_y[:, :, :-2])
    cond_z = jnp.pad(cond_mid, ((0, 0), (0, 0), (1, 1)))
    field_z = jnp.pad(centre, ((0, 0), (0, 0), (0, 0), (1, 1)))
    summed = summed + 0.5 * (cond_mid + cond_z[:, :, 2:]) * (centre - field_z[:, :, :, 2:])
    summed = summed + 0.5 * (cond_mid + cond_z[:, :, :-2]) * (centre - field_z[:, :, :, :-2])
    return summed


def bounds(shift_val, cond_max):
    high_eig = shift_val + 12.0 * cond_max
    mid_eig = 0.5 * (high_eig + shift_val)
    half_span = 0.5 * (high_eig - shift_val)
    return (mid_eig, half_span, mid_eig / half_span)


def solve_slabs(right_side, shift_val, cond_max, cond_ext):
    mid_eig, half_span, ratio_eig = bounds(shift_val, cond_max)
    rho_now = 1.0 / ratio_eig
    solution = jnp.zeros_like(right_side)
    residual = right_side
    direction = right_side / mid_eig
    for sweep_idx in range(STEPS - 1):
        solution = solution + direction
        padded = extended(direction, (("slab", 1),), 1)
        applied = conduction(padded, cond_ext) + shift_val * direction
        residual = residual - applied
        rho_next = 1.0 / (2.0 * ratio_eig - rho_now)
        direction = rho_next * rho_now * direction + 2.0 * rho_next / half_span * residual
        rho_now = rho_next
    return solution + direction


def run_segments(stacked, shifts, solver):
    factors = []
    current = stacked
    for segment_idx in range(ADI):
        shift_val = shifts[segment_idx]
        if segment_idx == 0:
            current = solver(stacked, shift_val)
        else:
            current = current - (shifts[segment_idx - 1] + shift_val) * solver(current, shift_val)
        factors.append(jnp.sqrt(2.0 * shift_val) * current)
    return jnp.stack(factors)


def body(input_map, output_map, region_ids, region_cond, shift_ids):
    col_local = input_map.shape[0]
    local_x = input_map.shape[1]
    cond_cells = lookup(region_ids, region_cond)
    cond_max = jnp.max(region_cond)
    shifts = 0.25 * jnp.exp2(shift_ids.astype(jnp.float32))
    total_x = local_x * lax.axis_size("slab")
    stacked = jnp.concatenate([input_map, output_map], 0)
    cond_ext = extended(cond_cells, (("slab", 0),), 1)
    factor_stack = run_segments(
        stacked, shifts, lambda rhs, shift_val: solve_slabs(rhs, shift_val, cond_max, cond_ext)
    )
    ctrl_local = factor_stack[:, :col_local]
    obsv_local = factor_stack[:, col_local:]
    ctrl_cols, obsv_cols = (
        lax.all_to_all(ctrl_local, "col", split_axis=3, concat_axis=1, tiled=True),
        lax.all_to_all(obsv_local, "col", split_axis=3, concat_axis=1, tiled=True),
    )
    row_count = ctrl_cols.shape[0] * ctrl_cols.shape[1]
    ctrl_flat = ctrl_cols.reshape(row_count, -1)
    obsv_flat = obsv_cols.reshape(row_count, -1)
    partial_value = lax.dot_general(
        ctrl_flat,
        obsv_flat,
        (((1,), (1,)), ((), ())),
        precision=lax.Precision.HIGHEST,
        preferred_element_type=jnp.float32,
    )
    cells_total = total_x * region_ids.shape[1] * region_ids.shape[2]
    norm_scale = 1.0 / math.sqrt(cells_total)
    whole_sum = lax.psum(partial_value, ("slab", "col"))
    tile_rows = row_count // lax.axis_size("slab")
    tile_cols = row_count // lax.axis_size("col")
    own_tile = lax.dynamic_slice(
        whole_sum,
        (lax.axis_index("slab") * tile_rows, lax.axis_index("col") * tile_cols),
        (tile_rows, tile_cols),
    )
    return (ctrl_cols, obsv_cols, own_tile * norm_scale)


def solution(mesh):
    placed = (
        P("col", "slab", None, None),
        P("col", "slab", None, None),
        P("slab", None, None),
        P(),
        P(),
    )
    return jax.shard_map(
        body,
        mesh=mesh,
        in_specs=placed,
        out_specs=(
            P(None, None, "slab", "col", None),
            P(None, None, "slab", "col", None),
            P("slab", "col"),
        ),
        check_vma=False,
    )
```

profile of v0, /device:TPU:1, one launch (start us, length us, event | category | flops | bytes accessed | tf_op | source)
XLA Modules:
  0.0 643.6 jit_solution(5252572299411760887)
XLA Ops:
  33.0 5.2 select_add_fusion
  44.6 22.0 %collective-permute-done = f32[1,192,128]{2,1,0:T(8,128)S(1)} collective-permute-done((f32[1,192,128]{2,1,0:T(8,128)S(1)}, f32[1,192,128]{2,1,0:T(8,128)S(1)}, u32[]{:S(2)}, u32[]{:S(2)}) %collective-permute-start) | collective-permute-done | bytes 98336 | tf_op jit(solution)/shard_map/ppermute | solution.py:19
  68.0 23.3 %multiply_add_fusion.1 = (f32[32,2,192,128]{3,2,1,0:T(8,128)S(1)}, f32[32,2,192,128]{3,2,1,0:T(8,128)}) fusion(f32[32,2,192,128]{3,2,1,0:T(8,128)} %copy-done.1, f32[]{:T(128)S(6)} %div.53, f32[]{:T(128)S(6)} %mul.354, f32[32,2,192,128]{3,2,1,0:T(8,128)} %constant_dynamic-update-slice_fusion, f32[]{:T(128)} %bitcast, ...), kind=kLoop, calls=%fused_computation.116 | loop fusion | flops 39321600 | bytes 32636940 | tf_op jit(solution)/shard_map/add | solution.py:66
  97.8 4.4 collective-permute-start.5
  103.6 32.0 %collective-permute-done.4 = f32[32,1,192,128]{3,2,1,0:T(8,128)} collective-permute-done((f32[32,1,192,128]{3,2,1,0:T(8,128)}, f32[32,1,192,128]{3,2,1,0:T(8,128)}, u32[]{:S(2)}, u32[]{:S(2)}) %collective-permute-start.4) | collective-permute-done | bytes 3145760 | tf_op jit(solution)/shard_map/ppermute | solution.py:19
  136.7 26.0 %broadcast_divide_fusion = (f32[32,2,192,128]{3,2,1,0:T(8,128)S(1)}, f32[32,2,192,128]{3,2,1,0:T(8,128)}) fusion(f32[]{:T(128)S(6)} %mul.397, f32[32,2,192,128]{3,2,1,0:T(8,128)} %get-tuple-element.8, f32[32,2,192,128]{3,2,1,0:T(8,128)} %copy-done.3, f32[]{:T(128)} %bitcast, f32[2,192,128]{2,1,0:T(8,128)S(1)} %get-tuple-element.29, ...), kind=kLoop, calls=%fused_computation.117 | loop fusion | flops 45613056 | bytes 38928404 | tf_op jit(solution)/shard_map/div | solution.py:59
  169.2 4.4 collective-permute-start.7
  175.1 31.8 %collective-permute-done.6 = f32[32,1,192,128]{3,2,1,0:T(8,128)} collective-permute-done((f32[32,1,192,128]{3,2,1,0:T(8,128)}, f32[32,1,192,128]{3,2,1,0:T(8,128)}, u32[]{:S(2)}, u32[]{:S(2)}) %collective-permute-start.6) | collective-permute-done | bytes 3145760 | tf_op jit(solution)/shard_map/ppermute | solution.py:19
  208.1 26.6 %multiply_add_fusion = (f32[32,2,192,128]{3,2,1,0:T(8,128)S(1)}, f32[32,2,192,128]{3,2,1,0:T(8,128)}, f32[1,32,2,192,128]{4,3,2,1,0:T(8,128)}) fusion(f32[]{:T(128)S(6)} %div.61, f32[]{:T(128)S(6)} %mul.400, f32[32,2,192,128]{3,2,1,0:T(8,128)} %get-tuple-element.6, f32[]{:T(128)S(6)} %mul.397, f32[32,2,192,128]{3,2,1,0:T(8,128)} %copy-done.2, f32[]{:T(128)} %bitcast.10, ...), kind=kLoop, calls=%fused_computation.114 | loop fusion | flops 42467328 | bytes 38928404 | tf_op jit(solution)/shard_map/add | solution.py:66
  241.2 4.6 collective-permute-start.9
  247.8 31.1 %collective-permute-done.8 = f32[32,1,192,128]{3,2,1,0:T(8,128)} collective-permute-done((f32[32,1,192,128]{3,2,1,0:T(8,128)}, f32[32,1,192,128]{3,2,1,0:T(8,128)}, u32[]{:S(2)}, u32[]{:S(2)}) %collective-permute-start.8) | collective-permute-done | bytes 3145760 | tf_op jit(solution)/shard_map/ppermute | solution.py:19
  280.1 27.0 %fusion.47 = f32[1,32,2,192,128]{4,3,2,1,0:T(8,128)S(1)} fusion(f32[32,2,192,128]{3,2,1,0:T(8,128)} %get-tuple-element.6, f32[32,2,192,128]{3,2,1,0:T(8,128)} %get-tuple-element.4, f32[32,2,192,128]{3,2,1,0:T(8,128)} %copy-done, f32[32,1,192,128]{3,2,1,0:T(8,128)} %collective-permute-done.9, f32[32,1,192,128]{3,2,1,0:T(8,128)} %collective-permute-done.8, ...), kind=kLoop, calls=%fused_computation.65 | loop fusion | flops 48758784 | bytes 32636952 | tf_op jit(solution)/shard_map/stack | solution.py:81
  310.3 7.6 %copy.32 = f32[2,16,2,192,128]{4,2,1,0,3:T(2,128)} copy(f32[2,16,2,192,128]{4,3,2,1,0:T(8,128)S(1)} %get-tuple-element.10) | data formatting | bytes 12582912 | tf_op jit(solution)/shard_map/slice | solution.py:96
  317.9 5.3 all-to-all-start
  323.1 10.2 %copy.34 = f32[2,16,2,192,128]{4,2,1,0,3:T(2,128)} copy(f32[2,16,2,192,128]{4,3,2,1,0:T(8,128)} %get-tuple-element.9) | data formatting | bytes 12582912 | tf_op jit(solution)/shard_map/slice | solution.py:97
  333.4 51.1 %all-to-all-done = f32[2,16,2,192,128]{4,2,1,0,3:T(2,128)} async-done(((f32[2,16,2,192,128]{4,2,1,0,3:T(2,128)}), f32[2,16,2,192,128]{4,2,1,0,3:T(2,128)}, u32[]{:S(2)}, u32[]{:S(2)}) %all-to-all-start) | async-done | bytes 6291488 | tf_op jit(solution)/shard_map/all_to_all | solution.py:99
  384.5 5.2 all-to-all-start.1
  390.0 9.0 %copy.41 = f32[2,16,2,4,48,128]{5,4,2,1,3,0:T(8,128)} copy(f32[2,16,2,4,48,128]{5,2,1,0,4,3:T(2,128)} %bitcast.12) | data formatting | bytes 12582912 | tf_op jit(solution)/shard_map/all_to_all | solution.py:99
  399.0 7.5 %reshape.20 = f32[128,12288]{1,0:T(8,128)} reshape(f32[2,4,16,2,48,128]{5,4,3,2,1,0:T(8,128)} %bitcast.32) | data formatting | bytes 12582912 | tf_op jit(solution)/shard_map/reshape | solution.py:103
  406.5 25.3 %all-to-all-done.1 = f32[2,16,2,192,128]{4,2,1,0,3:T(2,128)} async-done(((f32[2,16,2,192,128]{4,2,1,0,3:T(2,128)}), f32[2,16,2,192,128]{4,2,1,0,3:T(2,128)}, u32[]{:S(2)}, u32[]{:S(2)}) %all-to-all-start.1) | async-done | bytes 6291488 | tf_op jit(solution)/shard_map/all_to_all | solution.py:100
  431.7 9.0 %copy.40 = f32[2,16,2,4,48,128]{5,4,2,1,3,0:T(8,128)} copy(f32[2,16,2,4,48,128]{5,2,1,0,4,3:T(2,128)} %bitcast.15) | data formatting | bytes 12582912 | tf_op jit(solution)/shard_map/all_to_all | solution.py:100
  440.8 7.4 %reshape.21 = f32[128,12288]{1,0:T(8,128)} reshape(f32[2,4,16,2,48,128]{5,4,3,2,1,0:T(8,128)} %bitcast.34) | data formatting | bytes 12582912 | tf_op jit(solution)/shard_map/reshape | solution.py:104
  448.2 8.8 %fusion.109 = f32[128,128]{1,0:T(8,128)} fusion(f32[128,12288]{1,0:T(8,128)} %reshape.20, f32[128,12288]{1,0:T(8,128)} %reshape.21), kind=kOutput, calls=%fused_computation.151 | convolution fusion | flops 2415919104 | bytes 12648448 | tf_op jit(solution)/shard_map/dot_general | solution.py:105
  457.1 178.4 %all-reduce.12.cloned.1.call-done = f32[128,128]{1,0:T(8,128)} async-done(((f32[128,128]{1,0:T(8,128)}), f32[128,128]{1,0:T(8,128)}) %all-reduce.12.cloned.1.call-update) | async-done | bytes 65552 | tf_op jit(solution)/shard_map/psum | solution.py:114
  (46 shorter events, 58.6 us)
Async XLA Ops:
  7.2 8.6 %copy-start.5 = (f32[16,2,192,128]{3,2,1,0:T(8,128)S(1)}, f32[16,2,192,128]{3,2,1,0:T(8,128)}, u32[]{:S(2)}) copy-start(f32[16,2,192,128]{3,2,1,0:T(8,128)} %param.6) | copy-start | bytes 9437188
  20.9 4.6 copy-start.1
  20.9 11.4 %copy-start.7 = (f32[8]{0:T(128)S(1)}, f32[8]{0:T(128)}, u32[]{:S(2)}) copy-start(f32[8]{0:T(128)} %param.8) | copy-start | bytes 100
  20.9 12.1 %copy-start.6 = (s32[2,192,128]{2,1,0:T(8,128)S(1)}, s32[2,192,128]{2,1,0:T(8,128)}, u32[]{:S(2)}) copy-start(s32[2,192,128]{2,1,0:T(8,128)} %param.7) | copy-start | bytes 589828
  25.4 42.5 %collective-permute-start.1 = (f32[32,1,192,128]{3,2,1,0:T(8,128)}, f32[32,1,192,128]{3,2,1,0:T(8,128)}, u32[]{:S(2)}, u32[]{:S(2)}) collective-permute-start(f32[32,1,192,128]{3,2,1,0:T(8,128)} %get-tuple-element.22), channel_id=1, source_target_pairs={{4,0},{8,4},{12,8},{16,12},{20,16},{24,20},{28,24},{32,28},{36,32}... | collective-permute-start | bytes 9437192 | tf_op jit(solution)/shard_map/ppermute | solution.py:19
  28.8 39.2 %collective-permute-start.3 = (f32[32,1,192,128]{3,2,1,0:T(8,128)}, f32[32,1,192,128]{3,2,1,0:T(8,128)}, u32[]{:S(2)}, u32[]{:S(2)}) collective-permute-start(f32[32,1,192,128]{3,2,1,0:T(8,128)} %get-tuple-element.23), channel_id=1, source_target_pairs={{0,4},{4,8},{8,12},{12,16},{16,20},{20,24},{24,28},{28,32},{32,36}... | collective-permute-start | bytes 9437192 | tf_op jit(solution)/shard_map/ppermute | solution.py:16
  38.2 28.4 %collective-permute-start = (f32[1,192,128]{2,1,0:T(8,128)S(1)}, f32[1,192,128]{2,1,0:T(8,128)S(1)}, u32[]{:S(2)}, u32[]{:S(2)}) collective-permute-start(f32[1,192,128]{2,1,0:T(8,128)S(1)} %get-tuple-element.30), channel_id=1, source_target_pairs={{4,0},{8,4},{12,8},{16,12},{20,16},{24,20},{28,24},{32,28},{36,32}... | collective-permute-start | bytes 294920 | tf_op jit(solution)/shard_map/ppermute | solution.py:19
  40.7 27.1 %collective-permute-start.2 = (f32[1,192,128]{2,1,0:T(8,128)S(1)}, f32[1,192,128]{2,1,0:T(8,128)S(1)}, u32[]{:S(2)}, u32[]{:S(2)}) collective-permute-start(f32[1,192,128]{2,1,0:T(8,128)S(1)} %get-tuple-element.31), channel_id=1, source_target_pairs={{0,4},{4,8},{8,12},{12,16},{16,20},{20,24},{24,28},{28,32},{32,36}... | collective-permute-start | bytes 294920 | tf_op jit(solution)/shard_map/ppermute | solution.py:16
  91.3 4.6 copy-start.3
  95.9 39.6 %collective-permute-start.4 = (f32[32,1,192,128]{3,2,1,0:T(8,128)}, f32[32,1,192,128]{3,2,1,0:T(8,128)}, u32[]{:S(2)}, u32[]{:S(2)}) collective-permute-start(f32[32,1,192,128]{3,2,1,0:T(8,128)} %get-tuple-element.20), channel_id=1, source_target_pairs={{4,0},{8,4},{12,8},{16,12},{20,16},{24,20},{28,24},{32,28},{36,32}... | collective-permute-start | bytes 9437192 | tf_op jit(solution)/shard_map/ppermute | solution.py:19
  97.8 38.9 %collective-permute-start.5 = (f32[32,1,192,128]{3,2,1,0:T(8,128)}, f32[32,1,192,128]{3,2,1,0:T(8,128)}, u32[]{:S(2)}, u32[]{:S(2)}) collective-permute-start(f32[32,1,192,128]{3,2,1,0:T(8,128)} %get-tuple-element.21), channel_id=1, source_target_pairs={{0,4},{4,8},{8,12},{12,16},{16,20},{20,24},{24,28},{28,32},{32,36}... | collective-permute-start | bytes 9437192 | tf_op jit(solution)/shard_map/ppermute | solution.py:16
  162.7 4.6 copy-start.2
  167.3 39.6 %collective-permute-start.6 = (f32[32,1,192,128]{3,2,1,0:T(8,128)}, f32[32,1,192,128]{3,2,1,0:T(8,128)}, u32[]{:S(2)}, u32[]{:S(2)}) collective-permute-start(f32[32,1,192,128]{3,2,1,0:T(8,128)} %get-tuple-element.18), channel_id=1, source_target_pairs={{4,0},{8,4},{12,8},{16,12},{20,16},{24,20},{28,24},{32,28},{36,32}... | collective-permute-start | bytes 9437192 | tf_op jit(solution)/shard_map/ppermute | solution.py:19
  169.2 38.9 %collective-permute-start.7 = (f32[32,1,192,128]{3,2,1,0:T(8,128)}, f32[32,1,192,128]{3,2,1,0:T(8,128)}, u32[]{:S(2)}, u32[]{:S(2)}) collective-permute-start(f32[32,1,192,128]{3,2,1,0:T(8,128)} %get-tuple-element.19), channel_id=1, source_target_pairs={{0,4},{4,8},{8,12},{12,16},{16,20},{20,24},{24,28},{28,32},{32,36}... | collective-permute-start | bytes 9437192 | tf_op jit(solution)/shard_map/ppermute | solution.py:16
  234.7 4.6 copy-start
  239.3 39.6 %collective-permute-start.8 = (f32[32,1,192,128]{3,2,1,0:T(8,128)}, f32[32,1,192,128]{3,2,1,0:T(8,128)}, u32[]{:S(2)}, u32[]{:S(2)}) collective-permute-start(f32[32,1,192,128]{3,2,1,0:T(8,128)} %get-tuple-element.15), channel_id=1, source_target_pairs={{4,0},{8,4},{12,8},{16,12},{20,16},{24,20},{28,24},{32,28},{36,32}... | collective-permute-start | bytes 9437192 | tf_op jit(solution)/shard_map/ppermute | solution.py:19
  241.2 38.9 %collective-permute-start.9 = (f32[32,1,192,128]{3,2,1,0:T(8,128)}, f32[32,1,192,128]{3,2,1,0:T(8,128)}, u32[]{:S(2)}, u32[]{:S(2)}) collective-permute-start(f32[32,1,192,128]{3,2,1,0:T(8,128)} %get-tuple-element.16), channel_id=1, source_target_pairs={{0,4},{4,8},{8,12},{12,16},{16,20},{20,24},{24,28},{28,32},{32,36}... | collective-permute-start | bytes 9437192 | tf_op jit(solution)/shard_map/ppermute | solution.py:16
  280.1 27.0 %copy-start.4 = (f32[1,32,2,192,128]{4,3,2,1,0:T(8,128)S(1)}, f32[1,32,2,192,128]{4,3,2,1,0:T(8,128)}, u32[]{:S(2)}) copy-start(f32[1,32,2,192,128]{4,3,2,1,0:T(8,128)} %get-tuple-element.17) | copy-start | bytes 18874372
  317.9 66.6 %all-to-all-start = ((f32[2,16,2,192,128]{4,2,1,0,3:T(2,128)}), f32[2,16,2,192,128]{4,2,1,0,3:T(2,128)}, u32[]{:S(2)}, u32[]{:S(2)}) async-start(f32[2,16,2,192,128]{4,2,1,0,3:T(2,128)} %copy.32), calls=%async_computation | async-start | bytes 12582912 | tf_op jit(solution)/shard_map/all_to_all | solution.py:99
  384.5 47.3 %all-to-all-start.1 = ((f32[2,16,2,192,128]{4,2,1,0,3:T(2,128)}), f32[2,16,2,192,128]{4,2,1,0,3:T(2,128)}, u32[]{:S(2)}, u32[]{:S(2)}) async-start(f32[2,16,2,192,128]{4,2,1,0,3:T(2,128)} %copy.34), calls=%async_computation.1 | async-start | bytes 12582912 | tf_op jit(solution)/shard_map/all_to_all | solution.py:100
  389.7 245.7 %all-reduce.12.cloned.1.call-start = ((), (), s32[]{:S(2)}) async-start(), calls=%async_computation.2 | async-start | bytes 131072 | tf_op jit(solution)/shard_map/psum | solution.py:114
Sparse Core Ops, SparseCore 0:
  457.2 178.1 all-reduce.11
where the time goes:
time: 645 us; the launch traced here: 644 us
  waiting for transfers between devices  376 us (58%)
  other arithmetic  118 us (18%)
  local copies, waits for them, and re-layouts  76.2 us (12%)
  starting transfers between devices  42.3 us (7%)
  between operations  21.9 us (3%)
  matrix products  8.8 us (1%)
    psum x1, waiting for transfers between devices, body(): whole_sum = lax.psum(partial_value, ('slab', 'col'))  178 us
    ppermute x5, waiting for transfers between devices, extended(): lax.ppermute(lax.slice_in_dim(block, 0, width, axis=dim), axis, backward)  117 us
    all_to_all x1, waiting for transfers between devices, body(): lax.all_to_all(ctrl_local, 'col', split_axis=3, concat_axis=1, tiled=True)  51.1 us
    add x2, other arithmetic, solve_slabs(): rho_next * rho_now * direction + 2.0 * rho_next / half_span * residual  49.9 us
    another operation x2, other arithmetic, run_segments(): return jnp.stack(factors)  30.2 us
    div x2, other arithmetic, solve_slabs(): direction = right_side / mid_eig  29.2 us
    all_to_all x1, waiting for transfers between devices, body(): lax.all_to_all(obsv_local, 'col', split_axis=3, concat_axis=1, tiled=True)  25.3 us
    ppermute x5, starting transfers between devices, extended(): lax.ppermute(lax.slice_in_dim(block, block.shape[dim] - width, None, axis...  19.9 us
  transfers between devices with their start and end apart: 13, of which 11 were waited for; matrix products, arithmetic and copies ran while one was open for 5% of the time, Pallas kernels for 0%

commit v1 on v0

--- a/solution.py
+++ b/solution.py
@@ -111,7 +111,7 @@
     )
     cells_total = total_x * region_ids.shape[1] * region_ids.shape[2]
     norm_scale = 1.0 / math.sqrt(cells_total)
-    whole_sum = lax.psum(partial_value, ("slab", "col"))
+    whole_sum = jnp.sum(lax.all_gather(partial_value, ("slab", "col")), axis=0)
     tile_rows = row_count // lax.axis_size("slab")
     tile_cols = row_count // lax.axis_size("col")
     own_tile = lax.dynamic_slice(

time: 645 us -> 581 us (0.901)
  waiting for transfers between devices: 376 us -> 309 us
    psum x1 -> x0, waiting for transfers between devices: 178 us -> none  [body(): whole_sum = lax.psum(partial_value, ('slab', 'col'))]
    all_gather x0 -> x1, waiting for transfers between devices: none -> 111 us  [body(): whole_sum = jnp.sum(lax.all_gather(partial_value, ('slab', 'col')), axis=0)]
  transfers between devices with their start and end apart: 13 -> 13, of which waited for: 11 -> 11; matrix products, arithmetic and copies ran while one was open for 5% -> 6% of each run, Pallas kernels for 0% -> 0%
where the time goes in v1:
time: 581 us; the launch traced here: 579 us
  waiting for transfers between devices  309 us (53%)
  other arithmetic  121 us (21%)
  local copies, waits for them, and re-layouts  76.2 us (13%)
  starting transfers between devices  42.3 us (7%)
  between operations  21.9 us (4%)
  matrix products  8.8 us (2%)
    ppermute x5, waiting for transfers between devices, extended(): lax.ppermute(lax.slice_in_dim(block, 0, width, axis=dim), axis, backward)  117 us
    all_gather x1, waiting for transfers between devices, body(): whole_sum = jnp.sum(lax.all_gather(partial_value, ('slab', 'col')), axis=0)  111 us
    all_to_all x1, waiting for transfers between devices, body(): lax.all_to_all(ctrl_local, 'col', split_axis=3, concat_axis=1, tiled=True)  51.1 us
    add x2, other arithmetic, solve_slabs(): rho_next * rho_now * direction + 2.0 * rho_next / half_span * residual  49.9 us
    another operation x2, other arithmetic, run_segments(): return jnp.stack(factors)  30.2 us
    div x2, other arithmetic, solve_slabs(): direction = right_side / mid_eig  29.2 us
    all_to_all x1, waiting for transfers between devices, body(): lax.all_to_all(obsv_local, 'col', split_axis=3, concat_axis=1, tiled=True)  25.3 us
    ppermute x5, starting transfers between devices, extended(): lax.ppermute(lax.slice_in_dim(block, block.shape[dim] - width, None, axis...  19.9 us
  transfers between devices with their start and end apart: 13, of which 11 were waited for; matrix products, arithmetic and copies ran while one was open for 6% of the time, Pallas kernels for 0%

profile of v1, /device:TPU:1, one launch (start us, length us, event | category | flops | bytes accessed | tf_op | source)
XLA Modules:
  0.0 579.4 jit_solution(7154702397312808790)
XLA Ops:
  33.0 5.2 select_add_fusion
  44.6 22.0 %collective-permute-done = f32[1,192,128]{2,1,0:T(8,128)S(1)} collective-permute-done((f32[1,192,128]{2,1,0:T(8,128)S(1)}, f32[1,192,128]{2,1,0:T(8,128)S(1)}, u32[]{:S(2)}, u32[]{:S(2)}) %collective-permute-start) | collective-permute-done | bytes 98336 | tf_op jit(solution)/shard_map/ppermute | solution.py:19
  68.0 23.3 %multiply_add_fusion.1 = (f32[32,2,192,128]{3,2,1,0:T(8,128)S(1)}, f32[32,2,192,128]{3,2,1,0:T(8,128)}) fusion(f32[32,2,192,128]{3,2,1,0:T(8,128)} %copy-done.1, f32[]{:T(128)S(6)} %div.53, f32[]{:T(128)S(6)} %mul.354, f32[32,2,192,128]{3,2,1,0:T(8,128)} %constant_dynamic-update-slice_fusion, f32[]{:T(128)} %bitcast, ...), kind=kLoop, calls=%fused_computation.116 | loop fusion | flops 39321600 | bytes 32636940 | tf_op jit(solution)/shard_map/add | solution.py:66
  97.8 4.4 collective-permute-start.5
  103.6 32.0 %collective-permute-done.4 = f32[32,1,192,128]{3,2,1,0:T(8,128)} collective-permute-done((f32[32,1,192,128]{3,2,1,0:T(8,128)}, f32[32,1,192,128]{3,2,1,0:T(8,128)}, u32[]{:S(2)}, u32[]{:S(2)}) %collective-permute-start.4) | collective-permute-done | bytes 3145760 | tf_op jit(solution)/shard_map/ppermute | solution.py:19
  136.7 26.0 %broadcast_divide_fusion = (f32[32,2,192,128]{3,2,1,0:T(8,128)S(1)}, f32[32,2,192,128]{3,2,1,0:T(8,128)}) fusion(f32[]{:T(128)S(6)} %mul.397, f32[32,2,192,128]{3,2,1,0:T(8,128)} %get-tuple-element.8, f32[32,2,192,128]{3,2,1,0:T(8,128)} %copy-done.3, f32[]{:T(128)} %bitcast, f32[2,192,128]{2,1,0:T(8,128)S(1)} %get-tuple-element.29, ...), kind=kLoop, calls=%fused_computation.117 | loop fusion | flops 45613056 | bytes 38928404 | tf_op jit(solution)/shard_map/div | solution.py:59
  169.2 4.4 collective-permute-start.7
  175.1 31.8 %collective-permute-done.6 = f32[32,1,192,128]{3,2,1,0:T(8,128)} collective-permute-done((f32[32,1,192,128]{3,2,1,0:T(8,128)}, f32[32,1,192,128]{3,2,1,0:T(8,128)}, u32[]{:S(2)}, u32[]{:S(2)}) %collective-permute-start.6) | collective-permute-done | bytes 3145760 | tf_op jit(solution)/shard_map/ppermute | solution.py:19
  208.1 26.6 %multiply_add_fusion = (f32[32,2,192,128]{3,2,1,0:T(8,128)S(1)}, f32[32,2,192,128]{3,2,1,0:T(8,128)}, f32[1,32,2,192,128]{4,3,2,1,0:T(8,128)}) fusion(f32[]{:T(128)S(6)} %div.61, f32[]{:T(128)S(6)} %mul.400, f32[32,2,192,128]{3,2,1,0:T(8,128)} %get-tuple-element.6, f32[]{:T(128)S(6)} %mul.397, f32[32,2,192,128]{3,2,1,0:T(8,128)} %copy-done.2, f32[]{:T(128)} %bitcast.10, ...), kind=kLoop, calls=%fused_computation.114 | loop fusion | flops 42467328 | bytes 38928404 | tf_op jit(solution)/shard_map/add | solution.py:66
  241.2 4.6 collective-permute-start.9
  247.8 31.1 %collective-permute-done.8 = f32[32,1,192,128]{3,2,1,0:T(8,128)} collective-permute-done((f32[32,1,192,128]{3,2,1,0:T(8,128)}, f32[32,1,192,128]{3,2,1,0:T(8,128)}, u32[]{:S(2)}, u32[]{:S(2)}) %collective-permute-start.8) | collective-permute-done | bytes 3145760 | tf_op jit(solution)/shard_map/ppermute | solution.py:19
  280.1 27.0 %fusion.47 = f32[1,32,2,192,128]{4,3,2,1,0:T(8,128)S(1)} fusion(f32[32,2,192,128]{3,2,1,0:T(8,128)} %get-tuple-element.6, f32[32,2,192,128]{3,2,1,0:T(8,128)} %get-tuple-element.4, f32[32,2,192,128]{3,2,1,0:T(8,128)} %copy-done, f32[32,1,192,128]{3,2,1,0:T(8,128)} %collective-permute-done.9, f32[32,1,192,128]{3,2,1,0:T(8,128)} %collective-permute-done.8, ...), kind=kLoop, calls=%fused_computation.65 | loop fusion | flops 48758784 | bytes 32636952 | tf_op jit(solution)/shard_map/stack | solution.py:81
  310.3 7.6 %copy.32 = f32[2,16,2,192,128]{4,2,1,0,3:T(2,128)} copy(f32[2,16,2,192,128]{4,3,2,1,0:T(8,128)S(1)} %get-tuple-element.10) | data formatting | bytes 12582912 | tf_op jit(solution)/shard_map/slice | solution.py:96
  317.9 5.3 all-to-all-start
  323.1 10.2 %copy.34 = f32[2,16,2,192,128]{4,2,1,0,3:T(2,128)} copy(f32[2,16,2,192,128]{4,3,2,1,0:T(8,128)} %get-tuple-element.9) | data formatting | bytes 12582912 | tf_op jit(solution)/shard_map/slice | solution.py:97
  333.4 51.1 %all-to-all-done = f32[2,16,2,192,128]{4,2,1,0,3:T(2,128)} async-done(((f32[2,16,2,192,128]{4,2,1,0,3:T(2,128)}), f32[2,16,2,192,128]{4,2,1,0,3:T(2,128)}, u32[]{:S(2)}, u32[]{:S(2)}) %all-to-all-start) | async-done | bytes 6291488 | tf_op jit(solution)/shard_map/all_to_all | solution.py:99
  384.5 5.2 all-to-all-start.1
  390.0 9.0 %copy.41 = f32[2,16,2,4,48,128]{5,4,2,1,3,0:T(8,128)} copy(f32[2,16,2,4,48,128]{5,2,1,0,4,3:T(2,128)} %bitcast.12) | data formatting | bytes 12582912 | tf_op jit(solution)/shard_map/all_to_all | solution.py:99
  399.0 7.5 %reshape.20 = f32[128,12288]{1,0:T(8,128)} reshape(f32[2,4,16,2,48,128]{5,4,3,2,1,0:T(8,128)} %bitcast.33) | data formatting | bytes 12582912 | tf_op jit(solution)/shard_map/reshape | solution.py:103
  406.5 25.3 %all-to-all-done.1 = f32[2,16,2,192,128]{4,2,1,0,3:T(2,128)} async-done(((f32[2,16,2,192,128]{4,2,1,0,3:T(2,128)}), f32[2,16,2,192,128]{4,2,1,0,3:T(2,128)}, u32[]{:S(2)}, u32[]{:S(2)}) %all-to-all-start.1) | async-done | bytes 6291488 | tf_op jit(solution)/shard_map/all_to_all | solution.py:100
  431.7 9.0 %copy.40 = f32[2,16,2,4,48,128]{5,4,2,1,3,0:T(8,128)} copy(f32[2,16,2,4,48,128]{5,2,1,0,4,3:T(2,128)} %bitcast.15) | data formatting | bytes 12582912 | tf_op jit(solution)/shard_map/all_to_all | solution.py:100
  440.8 7.4 %reshape.21 = f32[128,12288]{1,0:T(8,128)} reshape(f32[2,4,16,2,48,128]{5,4,3,2,1,0:T(8,128)} %bitcast.35) | data formatting | bytes 12582912 | tf_op jit(solution)/shard_map/reshape | solution.py:104
  448.2 8.8 %fusion.109 = f32[128,128]{1,0:T(8,128)} fusion(f32[128,12288]{1,0:T(8,128)} %reshape.20, f32[128,12288]{1,0:T(8,128)} %reshape.21), kind=kOutput, calls=%fused_computation.151 | convolution fusion | flops 2415919104 | bytes 12648448 | tf_op jit(solution)/shard_map/dot_general | solution.py:105
  457.1 111.1 %all-gather.3.cloned.1.call-done = f32[16384,128]{1,0:T(8,128)} async-done(((f32[128,128]{1,0:T(8,128)}), f32[16384,128]{1,0:T(8,128)}) %all-gather.3.cloned.1.call-update) | async-done | bytes 8388624 | tf_op jit(solution)/shard_map/all_gather | solution.py:114
  (47 shorter events, 61.7 us)
Async XLA Ops:
  7.2 8.6 %copy-start.5 = (f32[16,2,192,128]{3,2,1,0:T(8,128)S(1)}, f32[16,2,192,128]{3,2,1,0:T(8,128)}, u32[]{:S(2)}) copy-start(f32[16,2,192,128]{3,2,1,0:T(8,128)} %param.6) | copy-start | bytes 9437188
  20.9 4.6 copy-start.1
  20.9 11.4 %copy-start.7 = (f32[8]{0:T(128)S(1)}, f32[8]{0:T(128)}, u32[]{:S(2)}) copy-start(f32[8]{0:T(128)} %param.8) | copy-start | bytes 100
  20.9 12.1 %copy-start.6 = (s32[2,192,128]{2,1,0:T(8,128)S(1)}, s32[2,192,128]{2,1,0:T(8,128)}, u32[]{:S(2)}) copy-start(s32[2,192,128]{2,1,0:T(8,128)} %param.7) | copy-start | bytes 589828
  25.4 42.5 %collective-permute-start.1 = (f32[32,1,192,128]{3,2,1,0:T(8,128)}, f32[32,1,192,128]{3,2,1,0:T(8,128)}, u32[]{:S(2)}, u32[]{:S(2)}) collective-permute-start(f32[32,1,192,128]{3,2,1,0:T(8,128)} %get-tuple-element.22), channel_id=1, source_target_pairs={{4,0},{8,4},{12,8},{16,12},{20,16},{24,20},{28,24},{32,28},{36,32}... | collective-permute-start | bytes 9437192 | tf_op jit(solution)/shard_map/ppermute | solution.py:19
  28.8 39.2 %collective-permute-start.3 = (f32[32,1,192,128]{3,2,1,0:T(8,128)}, f32[32,1,192,128]{3,2,1,0:T(8,128)}, u32[]{:S(2)}, u32[]{:S(2)}) collective-permute-start(f32[32,1,192,128]{3,2,1,0:T(8,128)} %get-tuple-element.23), channel_id=1, source_target_pairs={{0,4},{4,8},{8,12},{12,16},{16,20},{20,24},{24,28},{28,32},{32,36}... | collective-permute-start | bytes 9437192 | tf_op jit(solution)/shard_map/ppermute | solution.py:16
  38.2 28.4 %collective-permute-start = (f32[1,192,128]{2,1,0:T(8,128)S(1)}, f32[1,192,128]{2,1,0:T(8,128)S(1)}, u32[]{:S(2)}, u32[]{:S(2)}) collective-permute-start(f32[1,192,128]{2,1,0:T(8,128)S(1)} %get-tuple-element.30), channel_id=1, source_target_pairs={{4,0},{8,4},{12,8},{16,12},{20,16},{24,20},{28,24},{32,28},{36,32}... | collective-permute-start | bytes 294920 | tf_op jit(solution)/shard_map/ppermute | solution.py:19
  40.7 27.1 %collective-permute-start.2 = (f32[1,192,128]{2,1,0:T(8,128)S(1)}, f32[1,192,128]{2,1,0:T(8,128)S(1)}, u32[]{:S(2)}, u32[]{:S(2)}) collective-permute-start(f32[1,192,128]{2,1,0:T(8,128)S(1)} %get-tuple-element.31), channel_id=1, source_target_pairs={{0,4},{4,8},{8,12},{12,16},{16,20},{20,24},{24,28},{28,32},{32,36}... | collective-permute-start | bytes 294920 | tf_op jit(solution)/shard_map/ppermute | solution.py:16
  91.3 4.6 copy-start.3
  95.9 39.6 %collective-permute-start.4 = (f32[32,1,192,128]{3,2,1,0:T(8,128)}, f32[32,1,192,128]{3,2,1,0:T(8,128)}, u32[]{:S(2)}, u32[]{:S(2)}) collective-permute-start(f32[32,1,192,128]{3,2,1,0:T(8,128)} %get-tuple-element.20), channel_id=1, source_target_pairs={{4,0},{8,4},{12,8},{16,12},{20,16},{24,20},{28,24},{32,28},{36,32}... | collective-permute-start | bytes 9437192 | tf_op jit(solution)/shard_map/ppermute | solution.py:19
  97.8 38.9 %collective-permute-start.5 = (f32[32,1,192,128]{3,2,1,0:T(8,128)}, f32[32,1,192,128]{3,2,1,0:T(8,128)}, u32[]{:S(2)}, u32[]{:S(2)}) collective-permute-start(f32[32,1,192,128]{3,2,1,0:T(8,128)} %get-tuple-element.21), channel_id=1, source_target_pairs={{0,4},{4,8},{8,12},{12,16},{16,20},{20,24},{24,28},{28,32},{32,36}... | collective-permute-start | bytes 9437192 | tf_op jit(solution)/shard_map/ppermute | solution.py:16
  162.7 4.6 copy-start.2
  167.3 39.6 %collective-permute-start.6 = (f32[32,1,192,128]{3,2,1,0:T(8,128)}, f32[32,1,192,128]{3,2,1,0:T(8,128)}, u32[]{:S(2)}, u32[]{:S(2)}) collective-permute-start(f32[32,1,192,128]{3,2,1,0:T(8,128)} %get-tuple-element.18), channel_id=1, source_target_pairs={{4,0},{8,4},{12,8},{16,12},{20,16},{24,20},{28,24},{32,28},{36,32}... | collective-permute-start | bytes 9437192 | tf_op jit(solution)/shard_map/ppermute | solution.py:19
  169.2 38.9 %collective-permute-start.7 = (f32[32,1,192,128]{3,2,1,0:T(8,128)}, f32[32,1,192,128]{3,2,1,0:T(8,128)}, u32[]{:S(2)}, u32[]{:S(2)}) collective-permute-start(f32[32,1,192,128]{3,2,1,0:T(8,128)} %get-tuple-element.19), channel_id=1, source_target_pairs={{0,4},{4,8},{8,12},{12,16},{16,20},{20,24},{24,28},{28,32},{32,36}... | collective-permute-start | bytes 9437192 | tf_op jit(solution)/shard_map/ppermute | solution.py:16
  234.7 4.6 copy-start
  239.3 39.6 %collective-permute-start.8 = (f32[32,1,192,128]{3,2,1,0:T(8,128)}, f32[32,1,192,128]{3,2,1,0:T(8,128)}, u32[]{:S(2)}, u32[]{:S(2)}) collective-permute-start(f32[32,1,192,128]{3,2,1,0:T(8,128)} %get-tuple-element.15), channel_id=1, source_target_pairs={{4,0},{8,4},{12,8},{16,12},{20,16},{24,20},{28,24},{32,28},{36,32}... | collective-permute-start | bytes 9437192 | tf_op jit(solution)/shard_map/ppermute | solution.py:19
  241.2 38.9 %collective-permute-start.9 = (f32[32,1,192,128]{3,2,1,0:T(8,128)}, f32[32,1,192,128]{3,2,1,0:T(8,128)}, u32[]{:S(2)}, u32[]{:S(2)}) collective-permute-start(f32[32,1,192,128]{3,2,1,0:T(8,128)} %get-tuple-element.16), channel_id=1, source_target_pairs={{0,4},{4,8},{8,12},{12,16},{16,20},{20,24},{24,28},{28,32},{32,36}... | collective-permute-start | bytes 9437192 | tf_op jit(solution)/shard_map/ppermute | solution.py:16
  280.1 27.0 %copy-start.4 = (f32[1,32,2,192,128]{4,3,2,1,0:T(8,128)S(1)}, f32[1,32,2,192,128]{4,3,2,1,0:T(8,128)}, u32[]{:S(2)}) copy-start(f32[1,32,2,192,128]{4,3,2,1,0:T(8,128)} %get-tuple-element.17) | copy-start | bytes 18874372
  317.9 66.6 %all-to-all-start = ((f32[2,16,2,192,128]{4,2,1,0,3:T(2,128)}), f32[2,16,2,192,128]{4,2,1,0,3:T(2,128)}, u32[]{:S(2)}, u32[]{:S(2)}) async-start(f32[2,16,2,192,128]{4,2,1,0,3:T(2,128)} %copy.32), calls=%async_computation | async-start | bytes 12582912 | tf_op jit(solution)/shard_map/all_to_all | solution.py:99
  384.5 47.3 %all-to-all-start.1 = ((f32[2,16,2,192,128]{4,2,1,0,3:T(2,128)}), f32[2,16,2,192,128]{4,2,1,0,3:T(2,128)}, u32[]{:S(2)}, u32[]{:S(2)}) async-start(f32[2,16,2,192,128]{4,2,1,0,3:T(2,128)} %copy.34), calls=%async_computation.1 | async-start | bytes 12582912 | tf_op jit(solution)/shard_map/all_to_all | solution.py:100
  389.7 178.4 %all-gather.3.cloned.1.call-start = ((), (), s32[]{:S(2)}) async-start(), calls=%async_computation.2 | async-start | bytes 8454144 | tf_op jit(solution)/shard_map/all_gather | solution.py:114
Sparse Core Ops, SparseCore 0:
  457.2 110.8 all-gather.2
